TPU v7x, 32 devices: a whole 2x2x4 slice. The times are simulated.
32 devices in a mesh: sen: 8 (over z, y), par: 4 (over x, core).
Axes of the slice: x: 2, y: 2, z: 4, core: 2. Of those that a mesh axis runs over, the one named last changes fastest.
Arguments:
- vectors: float32 [3, 256, 420], P(None, ('par', 'sen')), may hold values from -6 to 6
- kernel: float32 [160, 256, 420], P('sen', 'par'), may hold values from -0.01953125 to 0.01953125
- noise: float32 [160, 420], P('sen'), may hold values from 0.25 to 4
Outputs:
- products: float32 [3, 256, 420], P(None, ('par', 'sen'))
All inputs are finite; a program needn't handle non-finite values.
Results may differ from a plain program's by a relative error of at most 0.0001.
Values sent between devices are 32-bit elements; how exact they have to be, the bound alone decides.
A program may use at most 128 MiB of HBM per device.

v0:
```python
import functools
import math

import jax
import jax.numpy as jnp
import numpy as np
from jax import lax
from jax.experimental import pallas as pl
from jax.experimental.pallas import tpu as pltpu
from jax.sharding import PartitionSpec as P

LANES = 128
MESH = pl.DeviceIdType.MESH


def round_up(value, step):
    return -(-value // step) * step


def make_tables(ntime):
    length = 2 * ntime
    nfreq = ntime + 1
    chunks = -(-nfreq // LANES)
    width = round_up(ntime, LANES)
    phase = np.arange(ntime)[:, None] * np.arange(nfreq)[None, :] % length
    angle = phase * (2.0 * math.pi / length)
    table = np.zeros((chunks, width, 2 * LANES), np.float64)
    factor = np.zeros((chunks, 1, 2 * LANES), np.float32)
    for c in range(chunks):
        freqs = np.arange(c * LANES, min((c + 1) * LANES, nfreq))
        table[c, :ntime, : len(freqs)] = np.cos(angle[:, freqs])
        table[c, :ntime, LANES : LANES + len(freqs)] = -np.sin(angle[:, freqs])
        weight = np.where((freqs == 0) | (freqs == ntime), 1.0, 2.0) / length
        factor[c, 0, : len(freqs)] = weight
        factor[c, 0, LANES : LANES + len(freqs)] = weight
    high = table.astype(np.float32).astype(jnp.bfloat16)
    low = (table - high.astype(np.float64)).astype(np.float32).astype(jnp.bfloat16)
    return high, low, factor


def split(x):
    high = x.astype(jnp.bfloat16)
    return high, (x - high.astype(jnp.float32)).astype(jnp.bfloat16)


def dot3(xh, xl, th, tl, transposed=False):
    dims = (((1,), (1 if transposed else 0,)), ((), ()))
    dot = functools.partial(lax.dot_general, dimension_numbers=dims, preferred_element_type=jnp.float32)
    return dot(xh, th) + dot(xh, tl) + dot(xl, th)


def body(n_sen, n_par, th, tl, fac, vec, kern, noise, out,
         xh, xl, spec, vg, vx, vhat, dhat, sig, sigr, what, ghat, gs, rs,
         vsend, vrecv, psend, precv, gsend, grecv):
    nvec, owned, ntime = vec.shape
    nsens, nsrc, _ = kern.shape
    chunks, width, _ = th.shape
    spad = round_up(nsens, 8)
    sen = lax.axis_index("sen")
    par = lax.axis_index("par")
    bits = n_par.bit_length() - 1
    partners = []
    for b in range(bits):
        w = 1 << b
        partners.append(par + (1 - 2 * ((par // w) % 2)) * w)

    barrier = pltpu.get_barrier_semaphore()
    for d in range(1, n_sen):
        pl.semaphore_signal(barrier, inc=1, device_id={"sen": (sen + d) % n_sen}, device_id_type=MESH)
    for p in partners:
        pl.semaphore_signal(barrier, inc=1, device_id={"par": p}, device_id_type=MESH)
    pl.semaphore_wait(barrier, n_sen - 1 + bits)

    def gather_copy(d):
        return pltpu.make_async_remote_copy(
            src_ref=vec, dst_ref=vg.at[sen], send_sem=vsend.at[d], recv_sem=vrecv.at[d],
            device_id={"sen": (sen + d) % n_sen}, device_id_type=MESH)

    for d in range(1, n_sen):
        gather_copy(d).start()
    vg[sen] = vec[...]

    tail = (ntime // LANES) * LANES
    if tail < width:
        xh[:, tail:] = jnp.zeros((nsens * nsrc, width - tail), jnp.bfloat16)
        xl[:, tail:] = jnp.zeros((nsens * nsrc, width - tail), jnp.bfloat16)
        vx[:, tail:] = jnp.zeros((nvec * nsrc, width - tail), jnp.float32)

    @pl.loop(0, nsens)
    def _(s):
        h, l = split(kern[s])
        rows = pl.ds(pl.multiple_of(s * nsrc, 16), nsrc)
        xh[rows, :ntime] = h
        xl[rows, :ntime] = l

    block = max(b for b in range(1, 11) if nsens % b == 0) * nsrc

    @pl.loop(0, chunks)
    def _(j):
        @pl.loop(0, nsens * nsrc // block)
        def _(m):
            rows = pl.ds(pl.multiple_of(m * block, 16), block)
            spec[j, rows, :] = dot3(xh[rows, :], xl[rows, :], th[j], tl[j])

    for d in range(1, n_sen):
        copy = gather_copy(d)
        copy.wait_send()
        copy.wait_recv()
    for o in range(n_sen):
        for v in range(nvec):
            vx[v * nsrc + o * owned : v * nsrc + (o + 1) * owned, :ntime] = vg[o, v]

    @pl.loop(0, chunks)
    def _(j):
        vhat[j] = dot3(*split(vx[...]), th[j], tl[j])

    dhat[...] = jnp.zeros(dhat.shape, jnp.float32)

    @pl.loop(0, chunks)
    def _(j):
        for s in range(nsens):
            rows = slice(s * nsrc, (s + 1) * nsrc)
            kr = spec[j, rows, :LANES]
            ki = spec[j, rows, LANES:]
            for v in range(nvec):
                vr = vhat[j, v * nsrc : (v + 1) * nsrc, :LANES]
                vi = vhat[j, v * nsrc : (v + 1) * nsrc, LANES:]
                row = slice(v * spad + s, v * spad + s + 1)
                dhat[j, row, :LANES] = jnp.sum(kr * vr - ki * vi, axis=0, keepdims=True)
                dhat[j, row, LANES:] = jnp.sum(kr * vi + ki * vr, axis=0, keepdims=True)

    signal = jnp.zeros((nvec * spad, width), jnp.float32)
    for j in range(chunks):
        signal = signal + dot3(*split(dhat[j] * fac[j]), th[j], tl[j], True)

    for b in range(bits):
        sig[b] = signal
        copy = pltpu.make_async_remote_copy(
            src_ref=sig.at[b], dst_ref=sigr.at[b], send_sem=psend.at[b], recv_sem=precv.at[b],
            device_id={"par": partners[b]}, device_id_type=MESH)
        copy.start()
        copy.wait()
        signal = sig[b] + sigr[b]

    sig[bits] = jnp.zeros((nvec * spad, width), jnp.float32)
    sig[bits] = signal
    for v in range(nvec):
        rows = slice(v * spad, v * spad + nsens)
        sig[bits, rows, :ntime] = sig[bits, rows, :ntime] * noise[...]

    @pl.loop(0, chunks)
    def _(j):
        what[j] = dot3(*split(sig[bits]), th[j], tl[j])

    step = math.gcd(nsrc, 32)

    @pl.loop(0, chunks)
    def _(j):
        @pl.loop(0, nsrc // step)
        def _(i):
            acc = [jnp.zeros((step, LANES), jnp.float32)] * (2 * nvec)
            for s in range(nsens):
                rows = pl.ds(pl.multiple_of(s * nsrc + i * step, 8), step)
                kr = spec[j, rows, :LANES]
                ki = spec[j, rows, LANES:]
                for v in range(nvec):
                    wr = what[j, v * spad + s : v * spad + s + 1, :LANES]
                    wi = what[j, v * spad + s : v * spad + s + 1, LANES:]
                    acc[2 * v] = acc[2 * v] + (kr * wr + ki * wi)
                    acc[2 * v + 1] = acc[2 * v + 1] + (kr * wi - ki * wr)
            for v in range(nvec):
                rows = pl.ds(pl.multiple_of(v * nsrc + i * step, 8), step)
                ghat[j, rows, :LANES] = acc[2 * v] * fac[j, :, :LANES]
                ghat[j, rows, LANES:] = acc[2 * v + 1] * fac[j, :, LANES:]

    grad = jnp.zeros((nvec * nsrc, width), jnp.float32)
    for j in range(chunks):
        grad = grad + dot3(*split(ghat[j]), th[j], tl[j], True)
    for o in range(n_sen):
        for v in range(nvec):
            gs[o, v * owned : (v + 1) * owned, :] = grad[v * nsrc + o * owned : v * nsrc + (o + 1) * owned]

    copies = []
    for d in range(1, n_sen):
        peer = (sen + d) % n_sen
        copies.append(pltpu.make_async_remote_copy(
            src_ref=gs.at[peer], dst_ref=rs.at[d], send_sem=gsend.at[d], recv_sem=grecv.at[d],
            device_id={"sen": peer}, device_id_type=MESH))
        copies[-1].start()
    total = gs[sen]
    for d in range(1, n_sen):
        copies[d - 1].wait()
        total = total + rs[d]
    for v in range(nvec):
        out[v] = total[v * owned : (v + 1) * owned, :ntime]


def per_device(n_sen, n_par, vectors, kernel, noise):
    nvec, owned, ntime = vectors.shape
    nsens, nsrc, _ = kernel.shape
    high, low, factor = make_tables(ntime)
    chunks, width, _ = high.shape
    spad = round_up(nsens, 8)
    bits = n_par.bit_length() - 1
    if n_par != 1 << bits:
        raise ValueError("par not 2^k")
    orow = round_up(nvec * owned, 8)
    f32, bf16 = jnp.float32, jnp.bfloat16
    vmem, dma = pltpu.VMEM, pltpu.SemaphoreType.DMA
    return pl.pallas_call(
        functools.partial(body, n_sen, n_par),
        out_shape=jax.ShapeDtypeStruct((nvec, owned, ntime), f32),
        in_specs=[pl.BlockSpec(memory_space=vmem)] * 6,
        out_specs=pl.BlockSpec(memory_space=vmem),
        scratch_shapes=[
            vmem((nsens * nsrc, width), bf16),
            vmem((nsens * nsrc, width), bf16),
            vmem((chunks, nsens * nsrc, 2 * LANES), f32),
            vmem((n_sen, nvec, owned, ntime), f32),
            vmem((nvec * nsrc, width), f32),
            vmem((chunks, nvec * nsrc, 2 * LANES), f32),
            vmem((chunks, nvec * spad, 2 * LANES), f32),
            vmem((bits + 1, nvec * spad, width), f32),
            vmem((max(bits, 1), nvec * spad, width), f32),
            vmem((chunks, nvec * spad, 2 * LANES), f32),
            vmem((chunks, nvec * nsrc, 2 * LANES), f32),
            vmem((n_sen, orow, width), f32),
            vmem((n_sen, orow, width), f32),
            dma((n_sen,)), dma((n_sen,)),
            dma((max(bits, 1),)), dma((max(bits, 1),)),
            dma((n_sen,)), dma((n_sen,)),
        ],
        compiler_params=pltpu.CompilerParams(
            collective_id=0, has_side_effects=True, vmem_limit_bytes=60 * 1024 * 1024),
    )(jnp.asarray(high), jnp.asarray(low), jnp.asarray(factor), vectors, kernel, noise)


def solution(mesh):
    n_sen, n_par = mesh.shape["sen"], mesh.shape["par"]
    return jax.shard_map(
        functools.partial(per_device, n_sen, n_par),
        mesh=mesh,
        in_specs=(P(None, ("par", "sen"), None), P("sen", "par", None), P("sen", None)),
        out_specs=P(None, ("par", "sen"), None),
        check_vma=False,
    )
```

profile of v0, /device:TPU:8, one launch (start us, length us, event | category | flops | bytes accessed | tf_op | source)
XLA Modules:
  0.0 44.0 jit_solution(10624520259861465203)
XLA Ops:
  0.0 42.6 %shard_map.64 = f32[3,8,420]{2,1,0:T(8,128)} custom-call(bf16[4,512,256]{2,1,0:T(8,128)(2,1)} %constant.6.clone.th, bf16[4,512,256]{2,1,0:T(8,128)(2,1)} %constant.7.clone.tl, f32[4,1,256]{2,1,0:T(1,128)} %constant.8.clone.fac, f32[3,8,420]{2,1,0:T(8,128)} %vec.1, f32[20,64,420]{2,1,0:T(8,128)} %kern.1, f32[20,420]{1,0:T(8,128)} %noise.1), custom_call_target="tpu_custom_call" | custom-call | tf_op jit(solution)/shard_map/pallas_call | solution.py:210
  42.6 1.4 %copy.8 = f32[3,8,420]{2,1,0:T(8,128)} copy(f32[3,8,420]{2,1,0:T(8,128)} %shard_map.64) | data formatting | bytes 80640
where the time goes:
time: 44.2 us; the launch traced here: 44 us
  Pallas kernels  42.6 us (96%)
  local copies, waits for them, and re-layouts  1.42 us (3%)
    pallas_call x1, Pallas kernels, per_device(): pl.pallas_call(functools.partial(body, n_sen, n_par), out_shape=jax.Shape...  42.6 us
    unnamed x1, local copies, waits for them, and re-layouts  1.42 us

commit v1 on v0

--- a/solution.py
+++ b/solution.py
@@ -49,63 +49,139 @@
     return dot(xh, th) + dot(xh, tl) + dot(xl, th)
 
 
-def body(n_sen, n_par, th, tl, fac, vec, kern, noise, out,
-         xh, xl, spec, vg, vx, vhat, dhat, sig, sigr, what, ghat, gs, rs,
-         vsend, vrecv, psend, precv, gsend, grecv):
+def inner_factor(count):
+    inner = 1
+    while count % (inner * 2) == 0 and (inner * 2) ** 2 <= count:
+        inner *= 2
+    return inner
+
+
+def sensor_block(nsens):
+    return max(b for b in range(1, 11) if nsens % b == 0)
+
+
+def body(n_sen, n_par, th_any, tl_any, fac, vec, kern_any, noise, out,
+         th, tl, kern, weight, xh, xl, spec, vg, vx, vhat, dhat, half, halfr, sig, sigr, full, what, ghat, gs, rs1, hs, rs2,
+         tsem, ksem, vsend, vrecv, wsend, wrecv, psend, precv, gsend, grecv, hsend, hrecv):
     nvec, owned, ntime = vec.shape
     nsens, nsrc, _ = kern.shape
     chunks, width, _ = th.shape
     spad = round_up(nsens, 8)
+    inner = inner_factor(n_sen)
+    outer = n_sen // inner
     sen = lax.axis_index("sen")
     par = lax.axis_index("par")
+    row, col = sen // inner, sen % inner
+    core = par % 2
     bits = n_par.bit_length() - 1
     partners = []
     for b in range(bits):
         w = 1 << b
         partners.append(par + (1 - 2 * ((par // w) % 2)) * w)
 
+    def on_row(d):
+        return ((row + d) % outer) * inner + col
+
+    def on_col(e):
+        return row * inner + (col + e) % inner
+
+    peers = [{"sen": on_row(d)} for d in range(1, outer)] + [{"sen": on_col(e)} for e in range(1, inner)]
+    peers += [{"par": p} for p in partners]
     barrier = pltpu.get_barrier_semaphore()
-    for d in range(1, n_sen):
-        pl.semaphore_signal(barrier, inc=1, device_id={"sen": (sen + d) % n_sen}, device_id_type=MESH)
-    for p in partners:
-        pl.semaphore_signal(barrier, inc=1, device_id={"par": p}, device_id_type=MESH)
-    pl.semaphore_wait(barrier, n_sen - 1 + bits)
-
-    def gather_copy(d):
-        return pltpu.make_async_remote_copy(
-            src_ref=vec, dst_ref=vg.at[sen], send_sem=vsend.at[d], recv_sem=vrecv.at[d],
-            device_id={"sen": (sen + d) % n_sen}, device_id_type=MESH)
-
-    for d in range(1, n_sen):
-        gather_copy(d).start()
-    vg[sen] = vec[...]
+    for peer in peers:
+        pl.semaphore_signal(barrier, inc=1, device_id=peer, device_id_type=MESH)
+
+    block = sensor_block(nsens)
+    pieces = nsens // block
+
+    def kern_copy(m):
+        part = pl.ds(m * block, block)
+        return pltpu.make_async_copy(kern_any.at[part], kern.at[part], ksem.at[m])
+
+    def table_copies(j):
+        return [pltpu.make_async_copy(th_any.at[j], th.at[j], tsem.at[0, j]),
+                pltpu.make_async_copy(tl_any.at[j], tl.at[j], tsem.at[1, j])]
+
+    def start_tables(j):
+        for copy in table_copies(j):
+            copy.start()
+
+    kern_copy(0).start()
+    start_tables(0)
+    for m in range(1, pieces):
+        kern_copy(m).start()
+    for j in range(1, chunks):
+        start_tables(j)
 
     tail = (ntime // LANES) * LANES
     if tail < width:
         xh[:, tail:] = jnp.zeros((nsens * nsrc, width - tail), jnp.bfloat16)
         xl[:, tail:] = jnp.zeros((nsens * nsrc, width - tail), jnp.bfloat16)
         vx[:, tail:] = jnp.zeros((nvec * nsrc, width - tail), jnp.float32)
-
-    @pl.loop(0, nsens)
-    def _(s):
-        h, l = split(kern[s])
-        rows = pl.ds(pl.multiple_of(s * nsrc, 16), nsrc)
-        xh[rows, :ntime] = h
-        xl[rows, :ntime] = l
-
-    block = max(b for b in range(1, 11) if nsens % b == 0) * nsrc
-
-    @pl.loop(0, chunks)
-    def _(j):
-        @pl.loop(0, nsens * nsrc // block)
+    dhat[...] = jnp.zeros(dhat.shape, jnp.float32)
+    weight[...] = jnp.zeros(weight.shape, jnp.float32)
+    weight[:nsens, :ntime] = noise[...]
+
+    pl.semaphore_wait(barrier, len(peers))
+
+    def row_copy(d):
+        return pltpu.make_async_remote_copy(
+            src_ref=vec, dst_ref=vg.at[sen], send_sem=vsend.at[d], recv_sem=vrecv.at[d],
+            device_id={"sen": on_row(d)}, device_id_type=MESH)
+
+    def col_copy(d, e):
+        owner = ((row + outer - d) % outer) * inner + col
+        return pltpu.make_async_remote_copy(
+            src_ref=vec if d == 0 else vg.at[owner], dst_ref=vg.at[owner],
+            send_sem=wsend.at[d, e], recv_sem=wrecv.at[d, e],
+            device_id={"sen": on_col(e)}, device_id_type=MESH)
+
+    def forward(d):
+        if d:
+            row_copy(d).wait_recv()
+        for e in range(1, inner):
+            col_copy(d, e).start()
+
+    order = sorted(range(outer), key=lambda d: (abs(d - outer / 2), d))
+    for d in order:
+        if d:
+            row_copy(d).start()
+    forward(0)
+    vg[sen] = vec[...]
+
+    for m in range(pieces):
+        kern_copy(m).wait()
+
+        @pl.loop(m * block, (m + 1) * block)
+        def _(s):
+            h, l = split(kern[s])
+            rows = pl.ds(pl.multiple_of(s * nsrc, 16), nsrc)
+            xh[rows, :ntime] = h
+            xl[rows, :ntime] = l
+
+    pending = list(range(1, outer))
+    for j in range(chunks):
+        for copy in table_copies(j):
+            copy.wait()
+
+        @pl.loop(0, pieces)
         def _(m):
-            rows = pl.ds(pl.multiple_of(m * block, 16), block)
+            rows = pl.ds(pl.multiple_of(m * block * nsrc, 16), block * nsrc)
             spec[j, rows, :] = dot3(xh[rows, :], xl[rows, :], th[j], tl[j])
 
-    for d in range(1, n_sen):
-        copy = gather_copy(d)
-        copy.wait_send()
-        copy.wait_recv()
+        left = chunks - 1 - j
+        count = -(-len(pending) // max(left, 1)) if j else 0
+        for d in pending[:count]:
+            forward(d)
+        pending = pending[count:]
+    for d in pending:
+        forward(d)
+
+    for d in range(1, outer):
+        row_copy(d).wait_send()
+    for d in range(outer):
+        for e in range(1, inner):
+            col_copy(d, e).wait()
     for o in range(n_sen):
         for v in range(nvec):
             vx[v * nsrc + o * owned : v * nsrc + (o + 1) * owned, :ntime] = vg[o, v]
@@ -113,8 +189,6 @@
     @pl.loop(0, chunks)
     def _(j):
         vhat[j] = dot3(*split(vx[...]), th[j], tl[j])
-
-    dhat[...] = jnp.zeros(dhat.shape, jnp.float32)
 
     @pl.loop(0, chunks)
     def _(j):
@@ -133,24 +207,30 @@
     for j in range(chunks):
         signal = signal + dot3(*split(dhat[j] * fac[j]), th[j], tl[j], True)
 
-    for b in range(bits):
-        sig[b] = signal
+    def exchange(b, src, dst, k):
         copy = pltpu.make_async_remote_copy(
-            src_ref=sig.at[b], dst_ref=sigr.at[b], send_sem=psend.at[b], recv_sem=precv.at[b],
+            src_ref=src, dst_ref=dst, send_sem=psend.at[k], recv_sem=precv.at[k],
             device_id={"par": partners[b]}, device_id_type=MESH)
         copy.start()
         copy.wait()
-        signal = sig[b] + sigr[b]
-
-    sig[bits] = jnp.zeros((nvec * spad, width), jnp.float32)
-    sig[bits] = signal
-    for v in range(nvec):
-        rows = slice(v * spad, v * spad + nsens)
-        sig[bits, rows, :ntime] = sig[bits, rows, :ntime] * noise[...]
+
+    half[0] = signal[:, : width // 2]
+    half[1] = signal[:, width // 2 :]
+    exchange(0, half.at[1 - core], halfr, bits)
+    acc = half[core] + halfr[...]
+    for b in range(1, bits):
+        sig[b] = acc
+        exchange(b, sig.at[b], sigr.at[b], b)
+        acc = sig[b] + sigr[b]
+    full[core] = acc
+    exchange(0, full.at[core], full.at[core], 0)
+    weighted = jnp.concatenate([full[0], full[1]], axis=1)
+    weighted = weighted * jnp.concatenate([weight[...]] * nvec, axis=0)
+    wh, wl = split(weighted)
 
     @pl.loop(0, chunks)
     def _(j):
-        what[j] = dot3(*split(sig[bits]), th[j], tl[j])
+        what[j] = dot3(wh, wl, th[j], tl[j])
 
     step = math.gcd(nsrc, 32)
 
@@ -180,17 +260,36 @@
         for v in range(nvec):
             gs[o, v * owned : (v + 1) * owned, :] = grad[v * nsrc + o * owned : v * nsrc + (o + 1) * owned]
 
-    copies = []
-    for d in range(1, n_sen):
-        peer = (sen + d) % n_sen
-        copies.append(pltpu.make_async_remote_copy(
-            src_ref=gs.at[peer], dst_ref=rs.at[d], send_sem=gsend.at[d], recv_sem=grecv.at[d],
-            device_id={"sen": peer}, device_id_type=MESH))
-        copies[-1].start()
-    total = gs[sen]
-    for d in range(1, n_sen):
-        copies[d - 1].wait()
-        total = total + rs[d]
+    def own_block(d, e):
+        return ((row + d) % outer) * inner + (col + e) % inner
+
+    def inner_copy(d, e):
+        return pltpu.make_async_remote_copy(
+            src_ref=gs.at[own_block(d, e)], dst_ref=rs1.at[d, e], send_sem=gsend.at[d, e], recv_sem=grecv.at[d, e],
+            device_id={"sen": on_col(e)}, device_id_type=MESH)
+
+    def outer_copy(d):
+        return pltpu.make_async_remote_copy(
+            src_ref=hs.at[d], dst_ref=rs2.at[d], send_sem=hsend.at[d], recv_sem=hrecv.at[d],
+            device_id={"sen": on_row(d)}, device_id_type=MESH)
+
+    for d in order:
+        for e in range(1, inner):
+            inner_copy(d, e).start()
+    for d in order:
+        part = gs[own_block(d, 0)]
+        for e in range(1, inner):
+            inner_copy(d, e).wait()
+            part = part + rs1[d, e]
+        if d:
+            hs[d] = part
+            outer_copy(d).start()
+        else:
+            total = part
+    for d in order:
+        if d:
+            outer_copy(d).wait()
+            total = total + rs2[d]
     for v in range(nvec):
         out[v] = total[v * owned : (v + 1) * owned, :ntime]
 
@@ -202,17 +301,23 @@
     chunks, width, _ = high.shape
     spad = round_up(nsens, 8)
     bits = n_par.bit_length() - 1
-    if n_par != 1 << bits:
+    if bits < 1 or n_par != 1 << bits:
         raise ValueError("par not 2^k")
     orow = round_up(nvec * owned, 8)
+    inner = inner_factor(n_sen)
+    outer = n_sen // inner
     f32, bf16 = jnp.float32, jnp.bfloat16
     vmem, dma = pltpu.VMEM, pltpu.SemaphoreType.DMA
     return pl.pallas_call(
         functools.partial(body, n_sen, n_par),
         out_shape=jax.ShapeDtypeStruct((nvec, owned, ntime), f32),
-        in_specs=[pl.BlockSpec(memory_space=vmem)] * 6,
+        in_specs=[pl.BlockSpec(memory_space=pl.ANY if i in (0, 1, 4) else vmem) for i in range(6)],
         out_specs=pl.BlockSpec(memory_space=vmem),
         scratch_shapes=[
+            vmem(high.shape, bf16),
+            vmem(low.shape, bf16),
+            vmem(kernel.shape, f32),
+            vmem((spad, width), f32),
             vmem((nsens * nsrc, width), bf16),
             vmem((nsens * nsrc, width), bf16),
             vmem((chunks, nsens * nsrc, 2 * LANES), f32),
@@ -220,15 +325,23 @@
             vmem((nvec * nsrc, width), f32),
             vmem((chunks, nvec * nsrc, 2 * LANES), f32),
             vmem((chunks, nvec * spad, 2 * LANES), f32),
-            vmem((bits + 1, nvec * spad, width), f32),
-            vmem((max(bits, 1), nvec * spad, width), f32),
+            vmem((2, nvec * spad, width // 2), f32),
+            vmem((nvec * spad, width // 2), f32),
+            vmem((bits, nvec * spad, width // 2), f32),
+            vmem((bits, nvec * spad, width // 2), f32),
+            vmem((2, nvec * spad, width // 2), f32),
             vmem((chunks, nvec * spad, 2 * LANES), f32),
             vmem((chunks, nvec * nsrc, 2 * LANES), f32),
             vmem((n_sen, orow, width), f32),
-            vmem((n_sen, orow, width), f32),
-            dma((n_sen,)), dma((n_sen,)),
-            dma((max(bits, 1),)), dma((max(bits, 1),)),
-            dma((n_sen,)), dma((n_sen,)),
+            vmem((outer, inner, orow, width), f32),
+            vmem((outer, orow, width), f32),
+            vmem((outer, orow, width), f32),
+            dma((2, chunks)), dma((nsens // sensor_block(nsens),)),
+            dma((outer,)), dma((outer,)),
+            dma((outer, inner)), dma((outer, inner)),
+            dma((bits + 1,)), dma((bits + 1,)),
+            dma((outer, inner)), dma((outer, inner)),
+            dma((outer,)), dma((outer,)),
         ],
         compiler_params=pltpu.CompilerParams(
             collective_id=0, has_side_effects=True, vmem_limit_bytes=60 * 1024 * 1024),

time: 44.2 us -> 42.9 us (0.971)
  the two profiles are of different devices: /device:TPU:8 before, /device:TPU:0 now
where the time goes in v1:
time: 42.9 us; the launch traced here: 42.7 us
  Pallas kernels  41.2 us (96%)
  local copies, waits for them, and re-layouts  1.42 us (3%)
    pallas_call x1, Pallas kernels, per_device(): pl.pallas_call(functools.partial(body, n_sen, n_par), out_shape=jax.Shape...  41.2 us
    unnamed x1, local copies, waits for them, and re-layouts  1.42 us

profile of v1, /device:TPU:0, one launch (start us, length us, event | category | flops | bytes accessed | tf_op | source)
XLA Modules:
  0.0 42.7 jit_solution(9582009846857840851)
XLA Ops:
  0.0 41.2 %shard_map.64 = f32[3,8,420]{2,1,0:T(8,128)} custom-call(bf16[4,512,256]{2,1,0:T(8,128)(2,1)} %constant.6.clone.th_any, bf16[4,512,256]{2,1,0:T(8,128)(2,1)} %constant.7.clone.tl_any, f32[4,1,256]{2,1,0:T(1,128)} %constant.8.clone.fac, f32[3,8,420]{2,1,0:T(8,128)} %vec.1, f32[20,64,420]{2,1,0:T(8,128)} %kern_any.1, f32[20,420]{1,0:T(8,128)} %noise.1), custom_call_target="tpu_custom_call" | custom-call | tf_op jit(solution)/shard_map/pallas_call | solution.py:311
  41.3 1.4 %copy.8 = f32[3,8,420]{2,1,0:T(8,128)} copy(f32[3,8,420]{2,1,0:T(8,128)} %shard_map.64) | data formatting | bytes 80640

commit v2 on v1

--- a/solution.py
+++ b/solution.py
@@ -43,8 +43,30 @@
     return high, (x - high.astype(jnp.float32)).astype(jnp.bfloat16)
 
 
-def dot3(xh, xl, th, tl, transposed=False):
-    dims = (((1,), (1 if transposed else 0,)), ((), ()))
+def packed_width(nvec, ntime):
+    whole = ntime // LANES * LANES
+    return nvec * whole + round_up(nvec * (ntime - whole), LANES)
+
+
+def spans(v, nvec, ntime):
+    whole = ntime // LANES * LANES
+    rest = ntime - whole
+    start = nvec * whole + v * rest
+    pairs = [(slice(0, whole), slice(v * whole, (v + 1) * whole)), (slice(whole, ntime), slice(start, start + rest))]
+    return [(a, b) for a, b in pairs if a.stop > a.start]
+
+
+def stack(x):
+    high, low = split(x)
+    return jnp.concatenate([high, low, high], axis=1)
+
+
+def dot(x, table):
+    return jnp.dot(x, table, preferred_element_type=jnp.float32)
+
+
+def dot3_transposed(xh, xl, th, tl):
+    dims = (((1,), (1,)), ((), ()))
     dot = functools.partial(lax.dot_general, dimension_numbers=dims, preferred_element_type=jnp.float32)
     return dot(xh, th) + dot(xh, tl) + dot(xl, th)
 
@@ -61,11 +83,11 @@
 
 
 def body(n_sen, n_par, th_any, tl_any, fac, vec, kern_any, noise, out,
-         th, tl, kern, weight, xh, xl, spec, vg, vx, vhat, dhat, half, halfr, sig, sigr, full, what, ghat, gs, rs1, hs, rs2,
+         tab, kern, weight, pack, x3, spec, vg, vx, vhat, dhat, half, halfr, sig, sigr, full, what, ghat, gs, rs1, hs, rs2,
          tsem, ksem, vsend, vrecv, wsend, wrecv, psend, precv, gsend, grecv, hsend, hrecv):
     nvec, owned, ntime = vec.shape
     nsens, nsrc, _ = kern.shape
-    chunks, width, _ = th.shape
+    chunks, width, _ = th_any.shape
     spad = round_up(nsens, 8)
     inner = inner_factor(n_sen)
     outer = n_sen // inner
@@ -99,8 +121,8 @@
         return pltpu.make_async_copy(kern_any.at[part], kern.at[part], ksem.at[m])
 
     def table_copies(j):
-        return [pltpu.make_async_copy(th_any.at[j], th.at[j], tsem.at[0, j]),
-                pltpu.make_async_copy(tl_any.at[j], tl.at[j], tsem.at[1, j])]
+        return [pltpu.make_async_copy(src.at[j], tab.at[j, pl.ds(i * width, width)], tsem.at[i, j])
+                for i, src in enumerate((th_any, th_any, tl_any))]
 
     def start_tables(j):
         for copy in table_copies(j):
@@ -115,10 +137,15 @@
 
     tail = (ntime // LANES) * LANES
     if tail < width:
-        xh[:, tail:] = jnp.zeros((nsens * nsrc, width - tail), jnp.bfloat16)
-        xl[:, tail:] = jnp.zeros((nsens * nsrc, width - tail), jnp.bfloat16)
+        for i in range(3):
+            x3[:, i * width + tail : (i + 1) * width] = jnp.zeros((nsens * nsrc, width - tail), jnp.bfloat16)
         vx[:, tail:] = jnp.zeros((nvec * nsrc, width - tail), jnp.float32)
     dhat[...] = jnp.zeros(dhat.shape, jnp.float32)
+    pack[...] = jnp.zeros(pack.shape, jnp.float32)
+    for v in range(nvec):
+        for columns, place in spans(v, nvec, ntime):
+            pack[:, place] = vec[v, :, columns]
+    gs[...] = jnp.zeros(gs.shape, jnp.float32)
     weight[...] = jnp.zeros(weight.shape, jnp.float32)
     weight[:nsens, :ntime] = noise[...]
 
@@ -126,13 +153,13 @@
 
     def row_copy(d):
         return pltpu.make_async_remote_copy(
-            src_ref=vec, dst_ref=vg.at[sen], send_sem=vsend.at[d], recv_sem=vrecv.at[d],
+            src_ref=pack, dst_ref=vg.at[sen], send_sem=vsend.at[d], recv_sem=vrecv.at[d],
             device_id={"sen": on_row(d)}, device_id_type=MESH)
 
     def col_copy(d, e):
         owner = ((row + outer - d) % outer) * inner + col
         return pltpu.make_async_remote_copy(
-            src_ref=vec if d == 0 else vg.at[owner], dst_ref=vg.at[owner],
+            src_ref=pack if d == 0 else vg.at[owner], dst_ref=vg.at[owner],
             send_sem=wsend.at[d, e], recv_sem=wrecv.at[d, e],
             device_id={"sen": on_col(e)}, device_id_type=MESH)
 
@@ -147,7 +174,7 @@
         if d:
             row_copy(d).start()
     forward(0)
-    vg[sen] = vec[...]
+    vg[sen] = pack[...]
 
     for m in range(pieces):
         kern_copy(m).wait()
@@ -156,8 +183,8 @@
         def _(s):
             h, l = split(kern[s])
             rows = pl.ds(pl.multiple_of(s * nsrc, 16), nsrc)
-            xh[rows, :ntime] = h
-            xl[rows, :ntime] = l
+            for i, part in enumerate((h, l, h)):
+                x3[rows, i * width : i * width + ntime] = part
 
     pending = list(range(1, outer))
     for j in range(chunks):
@@ -167,7 +194,7 @@
         @pl.loop(0, pieces)
         def _(m):
             rows = pl.ds(pl.multiple_of(m * block * nsrc, 16), block * nsrc)
-            spec[j, rows, :] = dot3(xh[rows, :], xl[rows, :], th[j], tl[j])
+            spec[j, rows, :] = dot(x3[rows, :], tab[j])
 
         left = chunks - 1 - j
         count = -(-len(pending) // max(left, 1)) if j else 0
@@ -184,11 +211,14 @@
             col_copy(d, e).wait()
     for o in range(n_sen):
         for v in range(nvec):
-            vx[v * nsrc + o * owned : v * nsrc + (o + 1) * owned, :ntime] = vg[o, v]
+            for columns, place in spans(v, nvec, ntime):
+                vx[v * nsrc + o * owned : v * nsrc + (o + 1) * owned, columns] = vg[o, :, place]
+
+    vstack = stack(vx[...])
 
     @pl.loop(0, chunks)
     def _(j):
-        vhat[j] = dot3(*split(vx[...]), th[j], tl[j])
+        vhat[j] = dot(vstack, tab[j])
 
     @pl.loop(0, chunks)
     def _(j):
@@ -205,7 +235,7 @@
 
     signal = jnp.zeros((nvec * spad, width), jnp.float32)
     for j in range(chunks):
-        signal = signal + dot3(*split(dhat[j] * fac[j]), th[j], tl[j], True)
+        signal = signal + dot3_transposed(*split(dhat[j] * fac[j]), tab[j, :width], tab[j, 2 * width :])
 
     def exchange(b, src, dst, k):
         copy = pltpu.make_async_remote_copy(
@@ -226,11 +256,11 @@
     exchange(0, full.at[core], full.at[core], 0)
     weighted = jnp.concatenate([full[0], full[1]], axis=1)
     weighted = weighted * jnp.concatenate([weight[...]] * nvec, axis=0)
-    wh, wl = split(weighted)
+    wstack = stack(weighted)
 
     @pl.loop(0, chunks)
     def _(j):
-        what[j] = dot3(wh, wl, th[j], tl[j])
+        what[j] = dot(wstack, tab[j])
 
     step = math.gcd(nsrc, 32)
 
@@ -255,10 +285,11 @@
 
     grad = jnp.zeros((nvec * nsrc, width), jnp.float32)
     for j in range(chunks):
-        grad = grad + dot3(*split(ghat[j]), th[j], tl[j], True)
+        grad = grad + dot3_transposed(*split(ghat[j]), tab[j, :width], tab[j, 2 * width :])
     for o in range(n_sen):
         for v in range(nvec):
-            gs[o, v * owned : (v + 1) * owned, :] = grad[v * nsrc + o * owned : v * nsrc + (o + 1) * owned]
+            for columns, place in spans(v, nvec, ntime):
+                gs[o, :, place] = grad[v * nsrc + o * owned : v * nsrc + (o + 1) * owned, columns]
 
     def own_block(d, e):
         return ((row + d) % outer) * inner + (col + e) % inner
@@ -291,7 +322,8 @@
             outer_copy(d).wait()
             total = total + rs2[d]
     for v in range(nvec):
-        out[v] = total[v * owned : (v + 1) * owned, :ntime]
+        for columns, place in spans(v, nvec, ntime):
+            out[v, :, columns] = total[:, place]
 
 
 def per_device(n_sen, n_par, vectors, kernel, noise):
@@ -303,7 +335,7 @@
     bits = n_par.bit_length() - 1
     if bits < 1 or n_par != 1 << bits:
         raise ValueError("par not 2^k")
-    orow = round_up(nvec * owned, 8)
+    packed = packed_width(nvec, ntime)
     inner = inner_factor(n_sen)
     outer = n_sen // inner
     f32, bf16 = jnp.float32, jnp.bfloat16
@@ -314,14 +346,13 @@
         in_specs=[pl.BlockSpec(memory_space=pl.ANY if i in (0, 1, 4) else vmem) for i in range(6)],
         out_specs=pl.BlockSpec(memory_space=vmem),
         scratch_shapes=[
-            vmem(high.shape, bf16),
-            vmem(low.shape, bf16),
+            vmem((chunks, 3 * width, 2 * LANES), bf16),
             vmem(kernel.shape, f32),
             vmem((spad, width), f32),
-            vmem((nsens * nsrc, width), bf16),
-            vmem((nsens * nsrc, width), bf16),
+            vmem((owned, packed), f32),
+            vmem((nsens * nsrc, 3 * width), bf16),
             vmem((chunks, nsens * nsrc, 2 * LANES), f32),
-            vmem((n_sen, nvec, owned, ntime), f32),
+            vmem((n_sen, owned, packed), f32),
             vmem((nvec * nsrc, width), f32),
             vmem((chunks, nvec * nsrc, 2 * LANES), f32),
             vmem((chunks, nvec * spad, 2 * LANES), f32),
@@ -332,11 +363,11 @@
             vmem((2, nvec * spad, width // 2), f32),
             vmem((chunks, nvec * spad, 2 * LANES), f32),
             vmem((chunks, nvec * nsrc, 2 * LANES), f32),
-            vmem((n_sen, orow, width), f32),
-            vmem((outer, inner, orow, width), f32),
-            vmem((outer, orow, width), f32),
-            vmem((outer, orow, width), f32),
-            dma((2, chunks)), dma((nsens // sensor_block(nsens),)),
+            vmem((n_sen, owned, packed), f32),
+            vmem((outer, inner, owned, packed), f32),
+            vmem((outer, owned, packed), f32),
+            vmem((outer, owned, packed), f32),
+            dma((3, chunks)), dma((nsens // sensor_block(nsens),)),
             dma((outer,)), dma((outer,)),
             dma((outer, inner)), dma((outer, inner)),
             dma((bits + 1,)), dma((bits + 1,)),

time: 42.9 us -> 41.7 us (0.972)
  Pallas kernels: 41.2 us -> 40 us
    pallas_call x1, Pallas kernels: 41.2 us -> 40 us  [per_device(): pl.pallas_call(functools.partial(body, n_sen, n_par), out_shape=jax.Shape...]
where the time goes in v2:
time: 41.7 us; the launch traced here: 41.5 us
  Pallas kernels  40 us (96%)
  local copies, waits for them, and re-layouts  1.42 us (3%)
    pallas_call x1, Pallas kernels, per_device(): pl.pallas_call(functools.partial(body, n_sen, n_par), out_shape=jax.Shape...  40 us
    unnamed x1, local copies, waits for them, and re-layouts  1.42 us

profile of v2, /device:TPU:0, one launch (start us, length us, event | category | flops | bytes accessed | tf_op | source)
XLA Modules:
  0.0 41.5 jit_solution(6680268772022443761)
XLA Ops:
  0.0 40.0 %shard_map.64 = f32[3,8,420]{2,1,0:T(8,128)} custom-call(bf16[4,512,256]{2,1,0:T(8,128)(2,1)} %constant.6.clone.th_any, bf16[4,512,256]{2,1,0:T(8,128)(2,1)} %constant.7.clone.tl_any, f32[4,1,256]{2,1,0:T(1,128)} %constant.8.clone.fac, f32[3,8,420]{2,1,0:T(8,128)} %vec.1, f32[20,64,420]{2,1,0:T(8,128)} %kern_any.1, f32[20,420]{1,0:T(8,128)} %noise.1), custom_call_target="tpu_custom_call" | custom-call | tf_op jit(solution)/shard_map/pallas_call | solution.py:343
  40.0 1.4 %copy.8 = f32[3,8,420]{2,1,0:T(8,128)} copy(f32[3,8,420]{2,1,0:T(8,128)} %shard_map.64) | data formatting | bytes 80640

commit v3 on v2

--- a/solution.py
+++ b/solution.py
@@ -186,7 +186,7 @@
             for i, part in enumerate((h, l, h)):
                 x3[rows, i * width : i * width + ntime] = part
 
-    pending = list(range(1, outer))
+    pending = [d for d in order if d]
     for j in range(chunks):
         for copy in table_copies(j):
             copy.wait()
@@ -197,7 +197,7 @@
             spec[j, rows, :] = dot(x3[rows, :], tab[j])
 
         left = chunks - 1 - j
-        count = -(-len(pending) // max(left, 1)) if j else 0
+        count = -(-len(pending) // max(left, 1))
         for d in pending[:count]:
             forward(d)
         pending = pending[count:]

time: 41.7 us -> 42.7 us (1.024)
  Pallas kernels: 40 us -> 41 us
    pallas_call x1, Pallas kernels: 40 us -> 41 us  [per_device(): pl.pallas_call(functools.partial(body, n_sen, n_par), out_shape=jax.Shape...]
where the time goes in v3:
time: 42.7 us; the launch traced here: 42.4 us
  Pallas kernels  41 us (96%)
  local copies, waits for them, and re-layouts  1.42 us (3%)
    pallas_call x1, Pallas kernels, per_device(): pl.pallas_call(functools.partial(body, n_sen, n_par), out_shape=jax.Shape...  41 us
    unnamed x1, local copies, waits for them, and re-layouts  1.42 us

profile of v3, /device:TPU:0, one launch (start us, length us, event | category | flops | bytes accessed | tf_op | source)
XLA Modules:
  0.0 42.4 jit_solution(4249443459370430472)
XLA Ops:
  0.0 41.0 %shard_map.64 = f32[3,8,420]{2,1,0:T(8,128)} custom-call(bf16[4,512,256]{2,1,0:T(8,128)(2,1)} %constant.6.clone.th_any, bf16[4,512,256]{2,1,0:T(8,128)(2,1)} %constant.7.clone.tl_any, f32[4,1,256]{2,1,0:T(1,128)} %constant.8.clone.fac, f32[3,8,420]{2,1,0:T(8,128)} %vec.1, f32[20,64,420]{2,1,0:T(8,128)} %kern_any.1, f32[20,420]{1,0:T(8,128)} %noise.1), custom_call_target="tpu_custom_call" | custom-call | tf_op jit(solution)/shard_map/pallas_call | solution.py:343
  41.0 1.4 %copy.8 = f32[3,8,420]{2,1,0:T(8,128)} copy(f32[3,8,420]{2,1,0:T(8,128)} %shard_map.64) | data formatting | bytes 80640
